TPU v7x, 32 devices: a whole 2x2x4 slice. The times are simulated.
32 devices in a mesh: dp: 8 (over z, y), mp: 4 (over x, core).
Axes of the slice: x: 2, y: 2, z: 4, core: 2. Of those that a mesh axis runs over, the one named last changes fastest.
Arguments:
- query: bfloat16 [4096, 4096], P('dp', 'mp'), may hold values from -6 to 6
- passage: bfloat16 [4096, 4096], P('dp', 'mp'), may hold values from -6 to 6
- query_scale: bfloat16 [4096], P('dp'), may hold values from 0.4 to 2.5
- passage_scale: bfloat16 [4096], P('dp'), may hold values from 0.4 to 2.5
- partners: int32 [8, 3], P('dp'), may hold values from 0 to 3, as said below
- counts: int32 [8], replicated, may hold values from 256 to 512, as said below
Outputs:
- loss: float32 [], replicated
- grad_query: bfloat16 [4096, 4096], P('dp', 'mp')
- grad_passage: bfloat16 [4096, 4096], P('dp', 'mp')
Inputs may be any that keep to these rules, and one draw needn't show every extreme that they name: `partners`: each nonzero entry of a row is a distinct distance; block 0 and the last 3 blocks use all 3 slots. `counts`: some block has all 512 rows valid.
All inputs are finite; a program needn't handle non-finite values.
Results may differ from a plain program's by a relative error of at most 0.004.
Values may be sent and summed in bfloat16 or wider, within the bound.
A program may use at most 64 MiB of HBM per device.

v0:
```python
import math
import jax
import jax.numpy as jnp
from jax import lax
from jax.sharding import PartitionSpec as P

D = 4096
WIN = 3


def shifted(value, axis, steps):
    count = lax.axis_size(axis)
    pairs = [(source, (source + steps) % count) for source in range(count)]
    return lax.ppermute(value, axis, pairs)


def local(query, passage, query_scale, passage_scale, partners, counts):
    inv = 1.0 / math.sqrt(D)
    rows = query.shape[0]
    mine = lax.axis_index("dp")
    ndev = lax.axis_size("dp")
    block_ids = jnp.arange(counts.shape[0], dtype=jnp.int32)

    def count_of(block):
        return jnp.sum(jnp.where(block_ids == block, counts, 0))

    far_rows = []
    far_scales = []
    far_counts = []
    for offset in range(1, WIN + 1):
        moved_rows, moved_scales = shifted((passage, passage_scale), "dp", -offset)
        far_rows.append(moved_rows)
        far_scales.append(moved_scales)
        far_counts.append(count_of((mine + offset) % ndev))
    offsets = partners[0]
    pick = jnp.clip(offsets - 1, 0, WIN - 1)
    keys = jnp.concatenate([passage[None], jnp.take(jnp.stack(far_rows), pick, axis=0)], axis=0)
    key_scales = jnp.concatenate(
        [passage_scale[None], jnp.take(jnp.stack(far_scales), pick, axis=0)], axis=0
    ).astype(jnp.float32)
    own_count = count_of(mine)
    key_counts = jnp.concatenate([own_count[None], jnp.take(jnp.stack(far_counts), pick)])
    live = jnp.concatenate([jnp.array([True]), offsets > 0])
    raw = jnp.einsum("id,kjd->kij", query, keys, preferred_element_type=jnp.float32)
    column = jnp.arange(rows, dtype=jnp.int32)
    col_ok = live[:, None] & (column[None, :] < key_counts[:, None])
    summed = lax.psum_scatter(raw, "mp", scatter_dimension=1, tiled=True)
    share = summed.shape[1]
    start = lax.axis_index("mp") * share
    row_ids = start + jnp.arange(share, dtype=jnp.int32)
    row_scale = lax.dynamic_slice_in_dim(query_scale, start, share).astype(jnp.float32)
    scores = summed * (row_scale * inv)[None, :, None] * key_scales[:, None, :]
    masked = jnp.where(col_ok[:, None, :], scores, -jnp.inf)
    top = jnp.max(masked, axis=(0, 2))
    weights = jnp.exp(masked - top[None, :, None])
    total = jnp.sum(weights, axis=(0, 2))
    lse = top + jnp.log(total)
    valid = row_ids < own_count
    diagonal = column[None, :] == row_ids[:, None]
    positive = jnp.sum(jnp.where(diagonal, scores[0], 0.0), axis=1)
    loss_rows = jnp.where(valid, lse - positive, 0.0)
    grads = weights / total[None, :, None]
    grads = jnp.concatenate([(grads[0] - diagonal.astype(jnp.float32))[None], grads[1:]], axis=0)
    grads = jnp.where(valid[None, :, None], grads, 0.0)
    key_weight = (grads * key_scales[:, None, :]).astype(jnp.bfloat16)
    row_weight = (grads * row_scale[None, :, None]).astype(jnp.bfloat16)
    loss_sum = jnp.sum(loss_rows)
    valid_sum = jnp.sum(valid.astype(jnp.float32))
    key_weight, row_weight = (
        lax.all_gather(key_weight, "mp", axis=1, tiled=True),
        lax.all_gather(row_weight, "mp", axis=1, tiled=True),
    )
    loss_all, valid_all = lax.psum((loss_sum, valid_sum), ("dp", "mp"))
    grad_query = jnp.einsum(
        "kij,kjd->id", key_weight, keys, preferred_element_type=jnp.float32
    ).astype(jnp.bfloat16)
    collected = jnp.einsum("ij,id->jd", row_weight[0], query, preferred_element_type=jnp.float32)
    far_parts = jnp.einsum(
        "kij,id->kjd", row_weight[1:], query, preferred_element_type=jnp.float32
    ).astype(jnp.bfloat16)
    for offset in range(1, WIN + 1):
        chosen = offsets == offset
        outgoing = jnp.sum(
            jnp.where(chosen[:, None, None], far_parts, jnp.zeros_like(far_parts)), axis=0
        )
        arrived = shifted(outgoing, "dp", offset)
        collected = collected + arrived.astype(jnp.float32)
    loss = loss_all / valid_all
    return (loss, grad_query, collected.astype(jnp.bfloat16))


def solution(mesh):
    return jax.shard_map(
        local,
        mesh=mesh,
        in_specs=(P("dp", "mp"), P("dp", "mp"), P("dp"), P("dp"), P("dp", None), P()),
        out_specs=(P(), P("dp", "mp"), P("dp", "mp")),
        check_vma=False,
    )
```

profile of v0, /device:TPU:0, one launch (start us, length us, event | category | flops | bytes accessed | tf_op | source)
XLA Modules:
  0.0 335.3 jit_solution(15261544324831672226)
XLA Ops:
  7.2 0.0 copy-start
  7.2 0.0 reduce-scatter.2.cloned.1.call-start
  7.2 5.1 %collective-permute-start.2 = (bf16[512,1024]{1,0:T(8,128)(2,1)}, bf16[512,1024]{1,0:T(8,128)(2,1)S(1)}, u32[]{:S(2)}, u32[]{:S(2)}) collective-permute-start(bf16[512,1024]{1,0:T(8,128)(2,1)} %param.8), channel_id=1, source_target_pairs={{0,20},{4,24},{8,28},{12,0},{16,4},{20,8},{24,12},{28,16},{1,21},{... | collective-permute-start | bytes 3145736 | tf_op jit(solution)/shard_map/ppermute | solution.py:14
  12.3 1.3 collective-permute-start.1
  13.6 0.5 collective-permute-start
  14.2 1.4 fusion.12
  15.6 2.1 pad_add_fusion.1
  17.6 0.7 fusion.15
  18.3 0.6 gather_fusion
  18.9 0.7 broadcast_select_fusion.2
  19.6 16.6 %collective-permute-done.2 = bf16[512,1024]{1,0:T(8,128)(2,1)S(1)} collective-permute-done((bf16[512,1024]{1,0:T(8,128)(2,1)}, bf16[512,1024]{1,0:T(8,128)(2,1)S(1)}, u32[]{:S(2)}, u32[]{:S(2)}) %collective-permute-start.2) | collective-permute-done | bytes 1048608 | tf_op jit(solution)/shard_map/ppermute | solution.py:14
  36.2 23.7 %collective-permute-done.1 = bf16[512,1024]{1,0:T(8,128)(2,1)S(1)} collective-permute-done((bf16[512,1024]{1,0:T(8,128)(2,1)}, bf16[512,1024]{1,0:T(8,128)(2,1)S(1)}, u32[]{:S(2)}, u32[]{:S(2)}) %collective-permute-start.1) | collective-permute-done | bytes 1048608 | tf_op jit(solution)/shard_map/ppermute | solution.py:14
  59.9 20.1 %collective-permute-done = bf16[512,1024]{1,0:T(8,128)(2,1)} collective-permute-done((bf16[512,1024]{1,0:T(8,128)(2,1)}, bf16[512,1024]{1,0:T(8,128)(2,1)}, u32[]{:S(2)}, u32[]{:S(2)}) %collective-permute-start) | collective-permute-done | bytes 1048608 | tf_op jit(solution)/shard_map/ppermute | solution.py:14
  80.0 3.2 pad_maximum_fusion.1
  83.2 4.4 %gather_fusion.1 = bf16[3,512,1024]{2,1,0:T(8,128)(2,1)} fusion(bf16[3,512,1024]{2,1,0:T(8,128)(2,1)} %pad_maximum_fusion.1, s32[1024]{0:T(1024)S(1)} %pad_clamp_fusion), kind=kCustom, calls=%fused_computation.1 | custom fusion | bytes 6291468 | tf_op jit(solution)/shard_map/jit(_take)/gather | solution.py:37
  87.7 0.0 copy-start.5
  87.7 2.3 broadcast_select_fusion
  90.0 0.0 copy-start.1
  90.0 1.7 copy-done.1
  91.7 0.0 copy-done
  91.7 0.0 copy-done.5
  91.7 4.3 %fusion.2 = f32[4,512,512]{1,2,0:T(8,128)} fusion(bf16[3,512,1024]{2,1,0:T(8,128)(2,1)S(1)} %broadcast_select_fusion, bf16[1,512,1024]{2,1,0:T(8,128)(2,1)S(1)} %bitcast.50, bf16[512,1024]{1,0:T(8,128)(2,1)S(1)} %copy-done), kind=kOutput, calls=%fused_computation.12 | convolution fusion | flops 2149580800 | bytes 9437184 | tf_op jit(solution)/shard_map/id,kjd->kij/dot_general | solution.py:44
  96.0 0.0 copy-start.3
  96.0 0.0 copy-start.2
  96.0 0.0 reduce-scatter.2.cloned.1.call-update
  96.1 0.0 all-gather.5.cloned.1.call-start
  96.1 0.6 copy-done.3
  96.7 3.3 collective-permute-start.5
  100.0 23.8 %collective-permute-start.4 = (bf16[512]{0:T(512)(128)(2,1)S(1)}, bf16[512]{0:T(512)(128)(2,1)S(1)}, u32[]{:S(2)}, u32[]{:S(2)}) collective-permute-start(bf16[512]{0:T(512)(128)(2,1)S(1)} %copy-done.3), channel_id=1, source_target_pairs={{0,24},{4,28},{8,0},{12,4},{16,8},{20,12},{24,16},{28,20},{1,25},{... | collective-permute-start | bytes 3080 | tf_op jit(solution)/shard_map/ppermute | solution.py:14
  123.8 0.7 collective-permute-start.3
  124.5 0.7 pad_add_fusion.2
  125.2 0.0 copy-done.2
  125.2 0.1 pad_add_fusion
  125.3 0.0 copy-done.4
  125.3 0.1 broadcast_multiply_fusion
  125.3 0.1 fusion.10
  125.4 0.0 collective-permute-done.5
  125.5 0.9 collective-permute-done.4
  126.4 1.0 collective-permute-done.3
  127.4 0.6 gather_fusion.2
  128.0 0.1 broadcast_select_fusion.1
  128.1 36.8 %reduce-scatter.2.cloned.1.call-done = f32[4,128,512]{1,2,0:T(8,128)} async-done(((f32[4,512,512]{1,2,0:T(8,128)}), f32[4,128,512]{1,2,0:T(8,128)}) %reduce-scatter.2.cloned.1.call-update) | async-done | bytes 1048592 | tf_op jit(solution)/shard_map/reduce_scatter | solution.py:47
  164.8 1.8 select_reduce_fusion.3
  166.6 0.1 fusion.9
  166.7 0.4 fusion.6
  167.1 0.5 fusion.5
  167.5 0.1 slice.28
  167.6 1.3 convert_reduce_fusion
  168.9 1.3 multiply_convert_fusion
  170.2 0.0 all-gather.5.cloned.1.call-update
  170.2 0.0 all-gather.3.cloned.1.call-start
  170.3 0.7 all-gather.3.cloned.1.call-update
  171.0 22.2 %all-gather.5.cloned.1.call-done = bf16[4,512,512]{1,2,0:T(8,128)(2,1)} async-done(((bf16[4,128,512]{1,2,0:T(8,128)(2,1)}), bf16[4,512,512]{1,2,0:T(8,128)(2,1)}) %all-gather.5.cloned.1.call-update) | async-done | bytes 2097168 | tf_op jit(solution)/shard_map/all_gather | solution.py:71
  193.2 5.5 %select_reduce_fusion.2 = (bf16[512,1024]{1,0:T(8,128)(2,1)S(1)}, bf16[512,1024]{1,0:T(8,128)(2,1)}, bf16[512,1024]{1,0:T(8,128)(2,1)}) fusion(pred[3]{0:T(512)(128)(4,1)S(1)} %get-tuple-element.24, pred[3]{0:T(512)(128)(4,1)S(1)} %get-tuple-element.26, pred[3]{0:T(512)(128)(4,1)S(1)} %get-tuple-element.23, ...), kind=kOutput, calls=%fused_computation.7 | convolution fusion | flops 1620049920 | bytes 6291465 | tf_op jit(solution)/shard_map/kij,id->kjd/dot_general | solution.py:78
  198.6 2.4 collective-permute-start.8
  201.0 1.5 collective-permute-start.7
  202.5 1.5 collective-permute-start.6
  204.0 112.5 %all-reduce = (f32[]{:T(128)}, f32[]{:T(128)}) all-reduce(f32[]{:T(128)} %get-tuple-element.7, f32[]{:T(128)} %get-tuple-element.6), channel_id=1, replica_groups=mesh['dp'=8,'mp'=4] {'dp','mp'}, use_global_device_ids=true, to_apply=%region_9.10 | all-reduce | flops 2 | bytes 16 | tf_op jit(solution)/shard_map/psum | solution.py:73
  317.8 0.0 all-gather.3.cloned.1.call-done
  317.9 5.9 %bitcast_convert_fusion = bf16[512,1024]{1,0:T(8,128)(2,1)} fusion(bf16[4,512,512]{1,2,0:T(8,128)(2,1)} %all-gather.3.cloned.1.call-done, bf16[3,512,1024]{2,1,0:T(8,128)(2,1)} %copy-done.1, bf16[1,512,1024]{2,1,0:T(8,128)(2,1)S(1)} %bitcast.51), kind=kOutput, calls=%fused_computation.13 | convolution fusion | flops 2150105088 | bytes 7340032 | tf_op jit(solution)/shard_map/kij,kjd->id/dot_general | solution.py:74
  323.7 0.0 collective-permute-done.8
  323.7 0.0 collective-permute-done.7
  323.7 0.0 collective-permute-done.6
  323.7 3.9 %add_convert_fusion = bf16[512,1024]{1,0:T(8,128)(2,1)} fusion(bf16[512,1024]{1,0:T(8,128)(2,1)} %collective-permute-done.8, bf16[512,1024]{1,0:T(8,128)(2,1)} %collective-permute-done.7, bf16[512,1024]{1,0:T(8,128)(2,1)} %collective-permute-done.6, bf16[512,1024]{1,0:T(8,128)(2,1)S(1)} %copy-done, bf16[4,512,512]{1,2,0:T(8,128)(2,1)} %all-gather.5.cloned.1.call-done), kind=kOutput, calls=%fused_computation.14 | convolution fusion | flops 540540928 | bytes 5767168 | tf_op jit(solution)/shard_map/ij,id->jd/dot_general | solution.py:77
  (11 shorter events, 0.1 us)
Async XLA Ops:
  7.2 84.6 %copy-start = (bf16[512,1024]{1,0:T(8,128)(2,1)S(1)}, bf16[512,1024]{1,0:T(8,128)(2,1)}, u32[]{:S(2)}) copy-start(bf16[512,1024]{1,0:T(8,128)(2,1)} %param.7) | copy-start | bytes 3145732
  7.2 157.7 %reduce-scatter.2.cloned.1.call-start = ((), (), s32[]{:S(2)}) async-start(), calls=%async_computation.1 | async-start | bytes 5242880 | tf_op jit(solution)/shard_map/reduce_scatter | solution.py:47
  7.2 29.0 %collective-permute-start.2 = (bf16[512,1024]{1,0:T(8,128)(2,1)}, bf16[512,1024]{1,0:T(8,128)(2,1)S(1)}, u32[]{:S(2)}, u32[]{:S(2)}) collective-permute-start(bf16[512,1024]{1,0:T(8,128)(2,1)} %param.8), channel_id=1, source_target_pairs={{0,20},{4,24},{8,28},{12,0},{16,4},{20,8},{24,12},{28,16},{1,21},{... | collective-permute-start | bytes 3145736 | tf_op jit(solution)/shard_map/ppermute | solution.py:14
  12.3 47.6 %collective-permute-start.1 = (bf16[512,1024]{1,0:T(8,128)(2,1)}, bf16[512,1024]{1,0:T(8,128)(2,1)S(1)}, u32[]{:S(2)}, u32[]{:S(2)}) collective-permute-start(bf16[512,1024]{1,0:T(8,128)(2,1)} %param.8), channel_id=1, source_target_pairs={{0,24},{4,28},{8,0},{12,4},{16,8},{20,12},{24,16},{28,20},{1,25},{... | collective-permute-start | bytes 3145736 | tf_op jit(solution)/shard_map/ppermute | solution.py:14
  13.6 66.4 %collective-permute-start = (bf16[512,1024]{1,0:T(8,128)(2,1)}, bf16[512,1024]{1,0:T(8,128)(2,1)}, u32[]{:S(2)}, u32[]{:S(2)}) collective-permute-start(bf16[512,1024]{1,0:T(8,128)(2,1)} %param.8), channel_id=1, source_target_pairs={{0,28},{4,0},{8,4},{12,8},{16,12},{20,16},{24,20},{28,24},{1,29},{... | collective-permute-start | bytes 3145736 | tf_op jit(solution)/shard_map/ppermute | solution.py:14
  87.7 4.0 %copy-start.5 = (bf16[512,1024]{1,0:T(8,128)(2,1)S(1)}, bf16[512,1024]{1,0:T(8,128)(2,1)}, u32[]{:S(2)}) copy-start(bf16[512,1024]{1,0:T(8,128)(2,1)} %param.8) | copy-start | bytes 3145732
  90.0 1.7 copy-start.1
  96.0 0.7 copy-start.3
  96.0 29.1 %copy-start.2 = (s32[1,3]{1,0:T(1,128)S(1)}, s32[1,3]{1,0:T(1,128)}, u32[]{:S(2)}) copy-start(s32[1,3]{1,0:T(1,128)} %param.11) | copy-start | bytes 40
  96.0 29.2 %copy-start.4 = (bf16[512]{0:T(512)(128)(2,1)S(1)}, bf16[512]{0:T(512)(128)(2,1)}, u32[]{:S(2)}) copy-start(bf16[512]{0:T(512)(128)(2,1)} %param.9) | copy-start | bytes 3076
  96.1 97.1 %all-gather.5.cloned.1.call-start = ((), (), s32[]{:S(2)}) async-start(), calls=%async_computation.3 | async-start | bytes 2621440 | tf_op jit(solution)/shard_map/all_gather | solution.py:71
  96.7 28.7 %collective-permute-start.5 = (bf16[512]{0:T(512)(128)(2,1)S(1)}, bf16[512]{0:T(512)(128)(2,1)S(1)}, u32[]{:S(2)}, u32[]{:S(2)}) collective-permute-start(bf16[512]{0:T(512)(128)(2,1)S(1)} %copy-done.3), channel_id=1, source_target_pairs={{0,20},{4,24},{8,28},{12,0},{16,4},{20,8},{24,12},{28,16},{1,21},{... | collective-permute-start | bytes 3080 | tf_op jit(solution)/shard_map/ppermute | solution.py:14
  100.0 26.4 %collective-permute-start.4 = (bf16[512]{0:T(512)(128)(2,1)S(1)}, bf16[512]{0:T(512)(128)(2,1)S(1)}, u32[]{:S(2)}, u32[]{:S(2)}) collective-permute-start(bf16[512]{0:T(512)(128)(2,1)S(1)} %copy-done.3), channel_id=1, source_target_pairs={{0,24},{4,28},{8,0},{12,4},{16,8},{20,12},{24,16},{28,20},{1,25},{... | collective-permute-start | bytes 3080 | tf_op jit(solution)/shard_map/ppermute | solution.py:14
  123.8 3.6 %collective-permute-start.3 = (bf16[512]{0:T(512)(128)(2,1)S(1)}, bf16[512]{0:T(512)(128)(2,1)S(1)}, u32[]{:S(2)}, u32[]{:S(2)}) collective-permute-start(bf16[512]{0:T(512)(128)(2,1)S(1)} %copy-done.3), channel_id=1, source_target_pairs={{0,28},{4,0},{8,4},{12,8},{16,12},{20,16},{24,20},{28,24},{1,29},{... | collective-permute-start | bytes 3080 | tf_op jit(solution)/shard_map/ppermute | solution.py:14
  170.2 147.7 %all-gather.3.cloned.1.call-start = ((), (), s32[]{:S(2)}) async-start(), calls=%async_computation.2 | async-start | bytes 2621440 | tf_op jit(solution)/shard_map/all_gather | solution.py:70
  198.6 125.1 %collective-permute-start.8 = (bf16[512,1024]{1,0:T(8,128)(2,1)}, bf16[512,1024]{1,0:T(8,128)(2,1)}, u32[]{:S(2)}, u32[]{:S(2)}) collective-permute-start(bf16[512,1024]{1,0:T(8,128)(2,1)} %get-tuple-element.4), channel_id=1, source_target_pairs={{0,12},{4,16},{8,20},{12,24},{16,28},{20,0},{24,4},{28,8},{1,13},{... | collective-permute-start | bytes 3145736 | tf_op jit(solution)/shard_map/ppermute | solution.py:14
  201.0 122.7 %collective-permute-start.7 = (bf16[512,1024]{1,0:T(8,128)(2,1)}, bf16[512,1024]{1,0:T(8,128)(2,1)}, u32[]{:S(2)}, u32[]{:S(2)}) collective-permute-start(bf16[512,1024]{1,0:T(8,128)(2,1)} %get-tuple-element.5), channel_id=1, source_target_pairs={{0,8},{4,12},{8,16},{12,20},{16,24},{20,28},{24,0},{28,4},{1,9},{5... | collective-permute-start | bytes 3145736 | tf_op jit(solution)/shard_map/ppermute | solution.py:14
  202.5 121.2 %collective-permute-start.6 = (bf16[512,1024]{1,0:T(8,128)(2,1)S(1)}, bf16[512,1024]{1,0:T(8,128)(2,1)}, u32[]{:S(2)}, u32[]{:S(2)}) collective-permute-start(bf16[512,1024]{1,0:T(8,128)(2,1)S(1)} %get-tuple-element.3), channel_id=1, source_target_pairs={{0,4},{4,8},{8,12},{12,16},{16,20},{20,24},{24,28},{28,0},{1,5},{5... | collective-permute-start | bytes 3145736 | tf_op jit(solution)/shard_map/ppermute | solution.py:14
Sparse Core Ops, SparseCore 0:
  96.2 68.6 reduce-scatter.1
  170.3 22.7 all-gather.4
  195.3 23.1 all-gather.2
where the time goes:
time: 336 us; the launch traced here: 335 us
  waiting for transfers between devices  122 us (36%)
  blocking collectives  112 us (33%)
  starting transfers between devices  40.1 us (12%)
  matrix products  19.5 us (6%)
  other arithmetic  16.7 us (5%)
  between operations  16.3 us (5%)
  local copies, waits for them, and re-layouts  8.01 us (2%)
    psum x1, blocking collectives, local(): loss_all, valid_all = lax.psum((loss_sum, valid_sum), ('dp', 'mp'))  112 us
    ppermute x9, waiting for transfers between devices, shifted(): return lax.ppermute(value, axis, pairs)  62.3 us
    ppermute x9, starting transfers between devices, shifted(): return lax.ppermute(value, axis, pairs)  40 us
    reduce_scatter x1, waiting for transfers between devices, local(): summed = lax.psum_scatter(raw, 'mp', scatter_dimension=1, tiled=True)  36.8 us
    all_gather x1, waiting for transfers between devices, local(): lax.all_gather(row_weight, 'mp', axis=1, tiled=True)  22.2 us
  transfers between devices with their start and end apart: 12, of which 7 were waited for; matrix products, arithmetic and copies ran while one was open for 5% of the time, Pallas kernels for 0%

commit v1 on v0

--- a/solution.py
+++ b/solution.py
@@ -70,7 +70,7 @@
         lax.all_gather(key_weight, "mp", axis=1, tiled=True),
         lax.all_gather(row_weight, "mp", axis=1, tiled=True),
     )
-    loss_all, valid_all = lax.psum((loss_sum, valid_sum), ("dp", "mp"))
+    loss_all, valid_all = lax.psum(lax.psum((loss_sum, valid_sum), "mp"), "dp")
     grad_query = jnp.einsum(
         "kij,kjd->id", key_weight, keys, preferred_element_type=jnp.float32
     ).astype(jnp.bfloat16)

time: 336 us -> 320 us (0.952); the launches traced: 335 us -> 315 us
  blocking collectives: 112 us -> 91.8 us
    psum x1 -> x2, blocking collectives: 112 us -> 91.8 us  [local(): loss_all, valid_all = lax.psum(lax.psum((loss_sum, valid_sum), 'mp'), 'dp')]
  transfers between devices with their start and end apart: 12 -> 12, of which waited for: 7 -> 7; matrix products, arithmetic and copies ran while one was open for 5% -> 6% of each run, Pallas kernels for 0% -> 0%
where the time goes in v1:
time: 320 us; the launch traced here: 315 us
  waiting for transfers between devices  122 us (38%)
  blocking collectives  91.8 us (29%)
  starting transfers between devices  40.1 us (13%)
  matrix products  19.5 us (6%)
  other arithmetic  16.7 us (5%)
  between operations  16.3 us (5%)
  local copies, waits for them, and re-layouts  8.01 us (3%)
    psum x2, blocking collectives, local(): loss_all, valid_all = lax.psum(lax.psum((loss_sum, valid_sum), 'mp'), 'dp')  91.8 us
    ppermute x9, waiting for transfers between devices, shifted(): return lax.ppermute(value, axis, pairs)  62.3 us
    ppermute x9, starting transfers between devices, shifted(): return lax.ppermute(value, axis, pairs)  40 us
    reduce_scatter x1, waiting for transfers between devices, local(): summed = lax.psum_scatter(raw, 'mp', scatter_dimension=1, tiled=True)  36.8 us
    all_gather x1, waiting for transfers between devices, local(): lax.all_gather(row_weight, 'mp', axis=1, tiled=True)  22.2 us
  transfers between devices with their start and end apart: 12, of which 7 were waited for; matrix products, arithmetic and copies ran while one was open for 6% of the time, Pallas kernels for 0%

profile of v1, /device:TPU:0, one launch (start us, length us, event | category | flops | bytes accessed | tf_op | source)
XLA Modules:
  0.0 314.6 jit_solution(11171668952502765720)
XLA Ops:
  7.2 0.0 copy-start
  7.2 0.0 reduce-scatter.2.cloned.1.call-start
  7.2 5.1 %collective-permute-start.2 = (bf16[512,1024]{1,0:T(8,128)(2,1)}, bf16[512,1024]{1,0:T(8,128)(2,1)S(1)}, u32[]{:S(2)}, u32[]{:S(2)}) collective-permute-start(bf16[512,1024]{1,0:T(8,128)(2,1)} %param.8), channel_id=1, source_target_pairs={{0,20},{4,24},{8,28},{12,0},{16,4},{20,8},{24,12},{28,16},{1,21},{... | collective-permute-start | bytes 3145736 | tf_op jit(solution)/shard_map/ppermute | solution.py:14
  12.3 1.3 collective-permute-start.1
  13.6 0.5 collective-permute-start
  14.2 1.4 fusion.12
  15.6 2.1 pad_add_fusion.1
  17.6 0.7 fusion.15
  18.3 0.6 gather_fusion
  18.9 0.7 broadcast_select_fusion.2
  19.6 16.6 %collective-permute-done.2 = bf16[512,1024]{1,0:T(8,128)(2,1)S(1)} collective-permute-done((bf16[512,1024]{1,0:T(8,128)(2,1)}, bf16[512,1024]{1,0:T(8,128)(2,1)S(1)}, u32[]{:S(2)}, u32[]{:S(2)}) %collective-permute-start.2) | collective-permute-done | bytes 1048608 | tf_op jit(solution)/shard_map/ppermute | solution.py:14
  36.2 23.7 %collective-permute-done.1 = bf16[512,1024]{1,0:T(8,128)(2,1)S(1)} collective-permute-done((bf16[512,1024]{1,0:T(8,128)(2,1)}, bf16[512,1024]{1,0:T(8,128)(2,1)S(1)}, u32[]{:S(2)}, u32[]{:S(2)}) %collective-permute-start.1) | collective-permute-done | bytes 1048608 | tf_op jit(solution)/shard_map/ppermute | solution.py:14
  59.9 20.1 %collective-permute-done = bf16[512,1024]{1,0:T(8,128)(2,1)} collective-permute-done((bf16[512,1024]{1,0:T(8,128)(2,1)}, bf16[512,1024]{1,0:T(8,128)(2,1)}, u32[]{:S(2)}, u32[]{:S(2)}) %collective-permute-start) | collective-permute-done | bytes 1048608 | tf_op jit(solution)/shard_map/ppermute | solution.py:14
  80.0 3.2 %pad_maximum_fusion.1 = bf16[3,512,1024]{2,1,0:T(8,128)(2,1)} fusion(bf16[1,512,1024]{2,1,0:T(8,128)(2,1)S(1)} %bitcast.48, bf16[1,512,1024]{2,1,0:T(8,128)(2,1)S(1)} %bitcast.49, bf16[1,512,1024]{2,1,0:T(8,128)(2,1)} %bitcast.9), kind=kLoop, calls=%fused_computation.4 | loop fusion | flops 3145728 | bytes 6291456 | tf_op jit(solution)/shard_map/stack | solution.py:37
  83.2 4.4 %gather_fusion.1 = bf16[3,512,1024]{2,1,0:T(8,128)(2,1)} fusion(bf16[3,512,1024]{2,1,0:T(8,128)(2,1)} %pad_maximum_fusion.1, s32[1024]{0:T(1024)S(1)} %pad_clamp_fusion), kind=kCustom, calls=%fused_computation.1 | custom fusion | bytes 6291468 | tf_op jit(solution)/shard_map/jit(_take)/gather | solution.py:37
  87.7 0.0 copy-start.5
  87.7 2.3 broadcast_select_fusion
  90.0 0.0 copy-start.1
  90.0 1.7 copy-done.1
  91.7 0.0 copy-done
  91.7 0.0 copy-done.5
  91.7 4.3 %fusion.2 = f32[4,512,512]{1,2,0:T(8,128)} fusion(bf16[3,512,1024]{2,1,0:T(8,128)(2,1)S(1)} %broadcast_select_fusion, bf16[1,512,1024]{2,1,0:T(8,128)(2,1)S(1)} %bitcast.50, bf16[512,1024]{1,0:T(8,128)(2,1)S(1)} %copy-done), kind=kOutput, calls=%fused_computation.12 | convolution fusion | flops 2149580800 | bytes 9437184 | tf_op jit(solution)/shard_map/id,kjd->kij/dot_general | solution.py:44
  96.0 0.0 copy-start.3
  96.0 0.0 reduce-scatter.2.cloned.1.call-update
  96.1 0.0 all-gather.5.cloned.1.call-start
  96.1 0.6 copy-done.3
  96.7 3.3 %collective-permute-start.5 = (bf16[512]{0:T(512)(128)(2,1)S(1)}, bf16[512]{0:T(512)(128)(2,1)S(1)}, u32[]{:S(2)}, u32[]{:S(2)}) collective-permute-start(bf16[512]{0:T(512)(128)(2,1)S(1)} %copy-done.3), channel_id=1, source_target_pairs={{0,20},{4,24},{8,28},{12,0},{16,4},{20,8},{24,12},{28,16},{1,21},{... | collective-permute-start | bytes 3080 | tf_op jit(solution)/shard_map/ppermute | solution.py:14
  100.0 23.8 %collective-permute-start.4 = (bf16[512]{0:T(512)(128)(2,1)S(1)}, bf16[512]{0:T(512)(128)(2,1)S(1)}, u32[]{:S(2)}, u32[]{:S(2)}) collective-permute-start(bf16[512]{0:T(512)(128)(2,1)S(1)} %copy-done.3), channel_id=1, source_target_pairs={{0,24},{4,28},{8,0},{12,4},{16,8},{20,12},{24,16},{28,20},{1,25},{... | collective-permute-start | bytes 3080 | tf_op jit(solution)/shard_map/ppermute | solution.py:14
  123.8 0.7 collective-permute-start.3
  124.5 0.7 pad_add_fusion.2
  125.2 0.0 copy-done.2
  125.2 0.1 pad_add_fusion
  125.3 0.0 copy-done.4
  125.3 0.1 broadcast_multiply_fusion
  125.3 0.1 fusion.10
  125.4 0.0 collective-permute-done.5
  125.5 0.9 collective-permute-done.4
  126.4 1.0 collective-permute-done.3
  127.4 0.6 gather_fusion.2
  128.0 0.1 broadcast_select_fusion.1
  128.1 36.8 %reduce-scatter.2.cloned.1.call-done = f32[4,128,512]{1,2,0:T(8,128)} async-done(((f32[4,512,512]{1,2,0:T(8,128)}), f32[4,128,512]{1,2,0:T(8,128)}) %reduce-scatter.2.cloned.1.call-update) | async-done | bytes 1048592 | tf_op jit(solution)/shard_map/reduce_scatter | solution.py:47
  164.8 1.8 select_reduce_fusion.3
  166.6 0.1 fusion.9
  166.7 0.4 fusion.6
  167.1 0.5 fusion.5
  167.5 0.1 slice.28
  167.6 1.3 convert_reduce_fusion
  168.9 1.3 multiply_convert_fusion
  170.2 0.0 all-gather.5.cloned.1.call-update
  170.2 0.0 all-gather.3.cloned.1.call-start
  170.3 0.7 all-gather.3.cloned.1.call-update
  170.9 22.2 %all-gather.5.cloned.1.call-done = bf16[4,512,512]{1,2,0:T(8,128)(2,1)} async-done(((bf16[4,128,512]{1,2,0:T(8,128)(2,1)}), bf16[4,512,512]{1,2,0:T(8,128)(2,1)}) %all-gather.5.cloned.1.call-update) | async-done | bytes 2097168 | tf_op jit(solution)/shard_map/all_gather | solution.py:71
  193.2 5.5 %select_reduce_fusion.2 = (bf16[512,1024]{1,0:T(8,128)(2,1)S(1)}, bf16[512,1024]{1,0:T(8,128)(2,1)}, bf16[512,1024]{1,0:T(8,128)(2,1)}) fusion(pred[3]{0:T(512)(128)(4,1)S(1)} %get-tuple-element.26, pred[3]{0:T(512)(128)(4,1)S(1)} %get-tuple-element.28, pred[3]{0:T(512)(128)(4,1)S(1)} %get-tuple-element.25, ...), kind=kOutput, calls=%fused_computation.7 | convolution fusion | flops 1620049920 | bytes 6291465 | tf_op jit(solution)/shard_map/kij,id->kjd/dot_general | solution.py:78
  198.6 2.4 collective-permute-start.8
  201.0 1.5 collective-permute-start.7
  202.5 1.5 collective-permute-start.6
  204.0 7.2 %all-reduce.1 = (f32[]{:T(128)}, f32[]{:T(128)}) all-reduce(f32[]{:T(128)} %get-tuple-element.7, f32[]{:T(128)} %get-tuple-element.6), channel_id=1, replica_groups=mesh['dp'=8,'mp'=4] {'mp'}, use_global_device_ids=true, to_apply=%region_9.10 | all-reduce | flops 2 | bytes 16 | tf_op jit(solution)/shard_map/psum | solution.py:73
  211.2 84.7 %all-reduce = (f32[]{:T(128)}, f32[]{:T(128)}) all-reduce(f32[]{:T(128)} %get-tuple-element.14, f32[]{:T(128)} %get-tuple-element.15), channel_id=1, replica_groups=mesh['dp'=8,'mp'=4] {'dp'}, use_global_device_ids=true, to_apply=%region_10.11 | all-reduce | flops 2 | bytes 16 | tf_op jit(solution)/shard_map/psum | solution.py:73
  297.1 0.0 all-gather.3.cloned.1.call-done
  297.1 5.9 %bitcast_convert_fusion = bf16[512,1024]{1,0:T(8,128)(2,1)} fusion(bf16[4,512,512]{1,2,0:T(8,128)(2,1)} %all-gather.3.cloned.1.call-done, bf16[3,512,1024]{2,1,0:T(8,128)(2,1)} %copy-done.1, bf16[1,512,1024]{2,1,0:T(8,128)(2,1)S(1)} %bitcast.51), kind=kOutput, calls=%fused_computation.13 | convolution fusion | flops 2150105088 | bytes 7340032 | tf_op jit(solution)/shard_map/kij,kjd->id/dot_general | solution.py:74
  303.0 0.0 collective-permute-done.8
  303.0 0.0 collective-permute-done.7
  303.0 0.0 collective-permute-done.6
  303.0 3.9 %add_convert_fusion = bf16[512,1024]{1,0:T(8,128)(2,1)} fusion(bf16[512,1024]{1,0:T(8,128)(2,1)} %collective-permute-done.8, bf16[512,1024]{1,0:T(8,128)(2,1)} %collective-permute-done.7, bf16[512,1024]{1,0:T(8,128)(2,1)} %collective-permute-done.6, bf16[512,1024]{1,0:T(8,128)(2,1)S(1)} %copy-done, bf16[4,512,512]{1,2,0:T(8,128)(2,1)} %all-gather.5.cloned.1.call-done), kind=kOutput, calls=%fused_computation.14 | convolution fusion | flops 540540928 | bytes 5767168 | tf_op jit(solution)/shard_map/ij,id->jd/dot_general | solution.py:77
  (12 shorter events, 0.1 us)
Async XLA Ops:
  7.2 84.6 %copy-start = (bf16[512,1024]{1,0:T(8,128)(2,1)S(1)}, bf16[512,1024]{1,0:T(8,128)(2,1)}, u32[]{:S(2)}) copy-start(bf16[512,1024]{1,0:T(8,128)(2,1)} %param.7) | copy-start | bytes 3145732
  7.2 157.7 %reduce-scatter.2.cloned.1.call-start = ((), (), s32[]{:S(2)}) async-start(), calls=%async_computation.1 | async-start | bytes 5242880 | tf_op jit(solution)/shard_map/reduce_scatter | solution.py:47
  7.2 29.0 %collective-permute-start.2 = (bf16[512,1024]{1,0:T(8,128)(2,1)}, bf16[512,1024]{1,0:T(8,128)(2,1)S(1)}, u32[]{:S(2)}, u32[]{:S(2)}) collective-permute-start(bf16[512,1024]{1,0:T(8,128)(2,1)} %param.8), channel_id=1, source_target_pairs={{0,20},{4,24},{8,28},{12,0},{16,4},{20,8},{24,12},{28,16},{1,21},{... | collective-permute-start | bytes 3145736 | tf_op jit(solution)/shard_map/ppermute | solution.py:14
  12.3 47.6 %collective-permute-start.1 = (bf16[512,1024]{1,0:T(8,128)(2,1)}, bf16[512,1024]{1,0:T(8,128)(2,1)S(1)}, u32[]{:S(2)}, u32[]{:S(2)}) collective-permute-start(bf16[512,1024]{1,0:T(8,128)(2,1)} %param.8), channel_id=1, source_target_pairs={{0,24},{4,28},{8,0},{12,4},{16,8},{20,12},{24,16},{28,20},{1,25},{... | collective-permute-start | bytes 3145736 | tf_op jit(solution)/shard_map/ppermute | solution.py:14
  13.6 66.4 %collective-permute-start = (bf16[512,1024]{1,0:T(8,128)(2,1)}, bf16[512,1024]{1,0:T(8,128)(2,1)}, u32[]{:S(2)}, u32[]{:S(2)}) collective-permute-start(bf16[512,1024]{1,0:T(8,128)(2,1)} %param.8), channel_id=1, source_target_pairs={{0,28},{4,0},{8,4},{12,8},{16,12},{20,16},{24,20},{28,24},{1,29},{... | collective-permute-start | bytes 3145736 | tf_op jit(solution)/shard_map/ppermute | solution.py:14
  87.7 4.0 %copy-start.5 = (bf16[512,1024]{1,0:T(8,128)(2,1)S(1)}, bf16[512,1024]{1,0:T(8,128)(2,1)}, u32[]{:S(2)}) copy-start(bf16[512,1024]{1,0:T(8,128)(2,1)} %param.8) | copy-start | bytes 3145732
  90.0 1.7 copy-start.1
  96.0 0.7 copy-start.3
  96.0 29.1 %copy-start.2 = (s32[1,3]{1,0:T(1,128)S(1)}, s32[1,3]{1,0:T(1,128)}, u32[]{:S(2)}) copy-start(s32[1,3]{1,0:T(1,128)} %param.11) | copy-start | bytes 40
  96.0 29.2 %copy-start.4 = (bf16[512]{0:T(512)(128)(2,1)S(1)}, bf16[512]{0:T(512)(128)(2,1)}, u32[]{:S(2)}) copy-start(bf16[512]{0:T(512)(128)(2,1)} %param.9) | copy-start | bytes 3076
  96.1 97.1 %all-gather.5.cloned.1.call-start = ((), (), s32[]{:S(2)}) async-start(), calls=%async_computation.3 | async-start | bytes 2621440 | tf_op jit(solution)/shard_map/all_gather | solution.py:71
  96.7 28.7 %collective-permute-start.5 = (bf16[512]{0:T(512)(128)(2,1)S(1)}, bf16[512]{0:T(512)(128)(2,1)S(1)}, u32[]{:S(2)}, u32[]{:S(2)}) collective-permute-start(bf16[512]{0:T(512)(128)(2,1)S(1)} %copy-done.3), channel_id=1, source_target_pairs={{0,20},{4,24},{8,28},{12,0},{16,4},{20,8},{24,12},{28,16},{1,21},{... | collective-permute-start | bytes 3080 | tf_op jit(solution)/shard_map/ppermute | solution.py:14
  100.0 26.4 %collective-permute-start.4 = (bf16[512]{0:T(512)(128)(2,1)S(1)}, bf16[512]{0:T(512)(128)(2,1)S(1)}, u32[]{:S(2)}, u32[]{:S(2)}) collective-permute-start(bf16[512]{0:T(512)(128)(2,1)S(1)} %copy-done.3), channel_id=1, source_target_pairs={{0,24},{4,28},{8,0},{12,4},{16,8},{20,12},{24,16},{28,20},{1,25},{... | collective-permute-start | bytes 3080 | tf_op jit(solution)/shard_map/ppermute | solution.py:14
  123.8 3.6 %collective-permute-start.3 = (bf16[512]{0:T(512)(128)(2,1)S(1)}, bf16[512]{0:T(512)(128)(2,1)S(1)}, u32[]{:S(2)}, u32[]{:S(2)}) collective-permute-start(bf16[512]{0:T(512)(128)(2,1)S(1)} %copy-done.3), channel_id=1, source_target_pairs={{0,28},{4,0},{8,4},{12,8},{16,12},{20,16},{24,20},{28,24},{1,29},{... | collective-permute-start | bytes 3080 | tf_op jit(solution)/shard_map/ppermute | solution.py:14
  170.2 126.9 %all-gather.3.cloned.1.call-start = ((), (), s32[]{:S(2)}) async-start(), calls=%async_computation.2 | async-start | bytes 2621440 | tf_op jit(solution)/shard_map/all_gather | solution.py:70
  198.6 104.4 %collective-permute-start.8 = (bf16[512,1024]{1,0:T(8,128)(2,1)}, bf16[512,1024]{1,0:T(8,128)(2,1)}, u32[]{:S(2)}, u32[]{:S(2)}) collective-permute-start(bf16[512,1024]{1,0:T(8,128)(2,1)} %get-tuple-element.4), channel_id=1, source_target_pairs={{0,12},{4,16},{8,20},{12,24},{16,28},{20,0},{24,4},{28,8},{1,13},{... | collective-permute-start | bytes 3145736 | tf_op jit(solution)/shard_map/ppermute | solution.py:14
  201.0 102.0 %collective-permute-start.7 = (bf16[512,1024]{1,0:T(8,128)(2,1)}, bf16[512,1024]{1,0:T(8,128)(2,1)}, u32[]{:S(2)}, u32[]{:S(2)}) collective-permute-start(bf16[512,1024]{1,0:T(8,128)(2,1)} %get-tuple-element.5), channel_id=1, source_target_pairs={{0,8},{4,12},{8,16},{12,20},{16,24},{20,28},{24,0},{28,4},{1,9},{5... | collective-permute-start | bytes 3145736 | tf_op jit(solution)/shard_map/ppermute | solution.py:14
  202.5 100.5 %collective-permute-start.6 = (bf16[512,1024]{1,0:T(8,128)(2,1)S(1)}, bf16[512,1024]{1,0:T(8,128)(2,1)}, u32[]{:S(2)}, u32[]{:S(2)}) collective-permute-start(bf16[512,1024]{1,0:T(8,128)(2,1)S(1)} %get-tuple-element.3), channel_id=1, source_target_pairs={{0,4},{4,8},{8,12},{12,16},{16,20},{20,24},{24,28},{28,0},{1,5},{5... | collective-permute-start | bytes 3145736 | tf_op jit(solution)/shard_map/ppermute | solution.py:14
Sparse Core Ops, SparseCore 0:
  96.2 68.6 reduce-scatter.1
  170.3 22.8 all-gather.4
  195.3 22.9 all-gather.2
